TPU v7x, 512 devices: a whole 4x4x16 slice. The times are simulated.
512 devices in a mesh: row: 32 (over z, y_lo), col: 16 (over y_hi, x, core).
Axes of the slice: x: 4, y: 4 (y_hi: 2, y_lo: 2; y = y_hi * 2 + y_lo), z: 16, core: 2. Of those that a mesh axis runs over, the one named last changes fastest.
Arguments:
- coords: int32 [3, 65536], P(None, ('row', 'col')), may hold values from 0 to 60809, as said below
- mode_shapes: bfloat16 [256, 65536], P(None, ('row', 'col')), as said below
- output_shapes: bfloat16 [1048576, 256], P(('row', 'col')), may hold values from -0.375 to 0.375
- response_gain: float32 [2, 256], replicated, may hold values from -4 to 4
Outputs:
- response_power: float32 [1048576], P(('row', 'col'))
- modal_csd: float32 [256, 256], replicated
Inputs may be any that keep to these rules, and one draw needn't show every extreme that they name: `coords`: positions of points on an aircraft's skin, numbered in no spatial order. `mode_shapes`: entries are of order 1 / sqrt(65536); each mode has a share of one sign over all nodes.
All inputs are finite; a program needn't handle non-finite values.
Results may differ from a plain program's by a relative error of at most 0.002.
Values may be sent and summed in bfloat16 or wider, within the bound.
A program may use at most 64 MiB of HBM per device.

v0:
```python
import math

import jax
import jax.numpy as jnp
from jax import lax
from jax.sharding import PartitionSpec as P

wave_scale = 0.35 / 64.0


def coherence(left_points, right_points):
    difference = (left_points[:, :, None] - right_points[:, None, :]).astype(jnp.float32)
    squared = jnp.sum(difference * difference, axis=0)
    return jnp.sinc(wave_scale * jnp.sqrt(squared)).astype(jnp.bfloat16)


def split_parts(matrix):
    high_part = matrix.astype(jnp.bfloat16)
    low_part = (matrix - high_part.astype(jnp.float32)).astype(jnp.bfloat16)
    return (high_part, low_part)


def modal_product(node_shapes, node_projection):
    high_part, low_part = split_parts(node_projection)
    dims = (((1,), (1,)), ((), ()))
    upper = lax.dot_general(node_shapes, high_part, dims, preferred_element_type=jnp.float32)
    lower = lax.dot_general(node_shapes, low_part, dims, preferred_element_type=jnp.float32)
    return upper + lower


def local(coords, mode_shapes, output_shapes, response_gain):
    row_shapes, row_points = (
        lax.all_gather(mode_shapes, "col", axis=1, tiled=True),
        lax.all_gather(coords, "col", axis=1, tiled=True),
    )
    mode_count = mode_shapes.shape[0]
    zero_block = jnp.zeros((mode_count, row_points.shape[1]), jnp.float32)
    piece_shapes = lax.all_gather(mode_shapes, "row", axis=1, tiled=True)
    piece_points = lax.all_gather(coords, "row", axis=1, tiled=True)
    length = piece_shapes.shape[1]
    block_size = math.gcd(length, 1024)
    block_count = length // block_size

    def add_block(loop_index, running_sum):
        block_start = loop_index * block_size
        part_shapes = lax.dynamic_slice_in_dim(piece_shapes, block_start, block_size, 1)
        part_points = lax.dynamic_slice_in_dim(piece_points, block_start, block_size, 1)
        coherence_tile = coherence(part_points, row_points)
        return running_sum + jnp.dot(
            part_shapes, coherence_tile, preferred_element_type=jnp.float32
        )

    projection = lax.fori_loop(0, block_count, add_block, zero_block)
    partial_csd = modal_product(row_shapes, projection)
    modal_csd = lax.psum(partial_csd, ("row", "col"))
    real_part = response_gain[0]
    imag_part = response_gain[1]
    weighted = (
        real_part[:, None] * real_part[None, :] + imag_part[:, None] * imag_part[None, :]
    ) * modal_csd
    weighted_high, weighted_low = split_parts(weighted)
    mapped = jnp.dot(output_shapes, weighted_high, preferred_element_type=jnp.float32)
    mapped = mapped + jnp.dot(output_shapes, weighted_low, preferred_element_type=jnp.float32)
    response_power = jnp.sum(mapped * output_shapes.astype(jnp.float32), axis=1)
    return (response_power, modal_csd)


def solution(mesh):
    in_specs = (P(None, ("row", "col")), P(None, ("row", "col")), P(("row", "col"), None), P())
    out_specs = (P(("row", "col")), P())
    return jax.shard_map(local, mesh=mesh, in_specs=in_specs, out_specs=out_specs, check_vma=False)
```

profile of v0, /device:TPU:1, one launch (start us, length us, event | category | flops | bytes accessed | tf_op | source)
XLA Modules:
  0.0 701.7 jit_solution(17819532380165018910)
XLA Ops:
  7.2 0.0 all-gather.3.cloned.1.call-start
  7.2 0.7 all-gather.3.cloned.1.call-update
  7.9 0.0 all-gather.5.cloned.1.call-start
  7.9 0.7 all-gather.5.cloned.1.call-update
  8.6 0.0 all-reduce.2.cloned.1.call-start
  8.7 57.3 %all_gather.13 = s32[3,4096]{1,0:T(4,128)S(1)} all-gather(s32[3,128]{1,0:T(4,128)} %param.6), channel_id=1, replica_groups=mesh['row'=32,'col'=16] {'row'}, dimensions={1}, use_global_device_ids=true | all-gather | bytes 50688 | tf_op jit(solution)/shard_map/all_gather | solution.py:39
  66.0 37.9 %all_gather.14 = s32[3,2048]{1,0:T(4,128)S(1)} all-gather(s32[3,128]{1,0:T(4,128)} %param.6), channel_id=1, replica_groups=mesh['row'=32,'col'=16] {'col'}, dimensions={1}, use_global_device_ids=true | all-gather | bytes 26112 | tf_op jit(solution)/shard_map/all_gather | solution.py:34
  104.0 2.3 copy.8
  106.3 23.6 %all-gather.3.cloned.1.call-done = bf16[256,4096]{1,0:T(8,128)(2,1)} async-done(((bf16[256,128]{1,0:T(8,128)(2,1)}), bf16[256,4096]{1,0:T(8,128)(2,1)}) %all-gather.3.cloned.1.call-update) | async-done | bytes 2097168 | tf_op jit(solution)/shard_map/all_gather | solution.py:38
  129.8 0.0 copy-start.1
  129.8 81.9 %while.16 = (s32[]{:T(128)}, f32[256,2048]{1,0:T(8,128)S(1)}, bf16[256,4096]{1,0:T(8,128)(2,1)}, s32[3,4096]{1,0:T(4,128)S(1)}, s32[3,2048]{1,0:T(4,128)S(1)}, /*index=5*/s32[]{:T(128)}, s32[]{:T(128)}, s32[]{:T(128)}, s32[]{:T(128)}) while((s32[]{:T(128)}, f32[256,2048]{1,0:T(8,128)S(1)}, bf16[256,4096]{1,0:T(8,128)(2,1)}, ...), condition=%wide.region_2.3_spmd.clone, body=%wide.region_0.2_spmd.clone.sunk | while | flops 1171259392 | bytes 21557404 | solution.py:53
  129.9 6.3 multiply_reduce_fusion.2
  136.2 14.1 %fusion.60 = f32[256,2048]{1,0:T(8,128)S(1)} fusion(f32[1024,2048]{1,0:T(8,128)} %multiply_reduce_fusion.2, f32[256,2048]{1,0:T(8,128)S(1)} %get-tuple-element.211, pred[]{:T(512)S(6)} %compare.3, bf16[256,4096]{1,0:T(8,128)(2,1)} %get-tuple-element.221, s32[]{:T(128)S(6)} %select_n.137), kind=kOutput, calls=%fused_computation.26.clone.1 | convolution fusion | flops 1148190720 | bytes 13107205 | tf_op jit(solution)/shard_map/while/body/eval_jaxpr/dot_general | solution.py:49
  150.3 6.3 multiply_reduce_fusion.2
  156.7 14.1 %fusion.60 = f32[256,2048]{1,0:T(8,128)S(1)} fusion(f32[1024,2048]{1,0:T(8,128)} %multiply_reduce_fusion.2, f32[256,2048]{1,0:T(8,128)S(1)} %get-tuple-element.211, pred[]{:T(512)S(6)} %compare.3, bf16[256,4096]{1,0:T(8,128)(2,1)} %get-tuple-element.221, s32[]{:T(128)S(6)} %select_n.137), kind=kOutput, calls=%fused_computation.26.clone.1 | convolution fusion | flops 1148190720 | bytes 13107205 | tf_op jit(solution)/shard_map/while/body/eval_jaxpr/dot_general | solution.py:49
  170.8 6.3 multiply_reduce_fusion.2
  177.2 14.1 %fusion.60 = f32[256,2048]{1,0:T(8,128)S(1)} fusion(f32[1024,2048]{1,0:T(8,128)} %multiply_reduce_fusion.2, f32[256,2048]{1,0:T(8,128)S(1)} %get-tuple-element.211, pred[]{:T(512)S(6)} %compare.3, bf16[256,4096]{1,0:T(8,128)(2,1)} %get-tuple-element.221, s32[]{:T(128)S(6)} %select_n.137), kind=kOutput, calls=%fused_computation.26.clone.1 | convolution fusion | flops 1148190720 | bytes 13107205 | tf_op jit(solution)/shard_map/while/body/eval_jaxpr/dot_general | solution.py:49
  191.3 6.3 multiply_reduce_fusion.2
  197.6 14.1 %fusion.60 = f32[256,2048]{1,0:T(8,128)S(1)} fusion(f32[1024,2048]{1,0:T(8,128)} %multiply_reduce_fusion.2, f32[256,2048]{1,0:T(8,128)S(1)} %get-tuple-element.211, pred[]{:T(512)S(6)} %compare.3, bf16[256,4096]{1,0:T(8,128)(2,1)} %get-tuple-element.221, s32[]{:T(128)S(6)} %select_n.137), kind=kOutput, calls=%fused_computation.26.clone.1 | convolution fusion | flops 1148190720 | bytes 13107205 | tf_op jit(solution)/shard_map/while/body/eval_jaxpr/dot_general | solution.py:49
  211.8 0.0 copy-start
  211.8 0.0 all-gather.5.cloned.1.call-done
  211.8 1.8 fusion.37
  213.6 2.4 fusion.35
  216.0 0.0 all-reduce.2.cloned.1.call-update
  216.0 0.0 copy-done.1
  216.1 473.4 %all-reduce.2.cloned.1.call-done = f32[256,256]{0,1:T(8,128)} async-done(((f32[256,256]{0,1:T(8,128)}), f32[256,256]{0,1:T(8,128)}) %all-reduce.2.cloned.1.call-update) | async-done | bytes 262160 | tf_op jit(solution)/shard_map/psum | solution.py:55
  689.5 1.8 copy.9
  691.3 0.0 copy-done
  691.3 1.4 fusion.40
  692.7 2.5 fusion.34
  (6 shorter events, 0.0 us)
Async XLA Ops:
  7.2 122.7 %all-gather.3.cloned.1.call-start = ((), (), s32[]{:S(2)}) async-start(), calls=%async_computation | async-start | bytes 2162688 | tf_op jit(solution)/shard_map/all_gather | solution.py:38
  7.9 203.9 %all-gather.5.cloned.1.call-start = ((), (), s32[]{:S(2)}) async-start(), calls=%async_computation.1 | async-start | bytes 1114112 | tf_op jit(solution)/shard_map/all_gather | solution.py:33
  8.6 680.8 %all-reduce.2.cloned.1.call-start = ((), (), s32[]{:S(2)}) async-start(), calls=%async_computation.2 | async-start | bytes 524288 | tf_op jit(solution)/shard_map/psum | solution.py:55
  129.8 86.2 %copy-start.1 = (f32[2,256]{1,0:T(2,128)S(1)}, f32[2,256]{1,0:T(2,128)}, u32[]{:S(2)}) copy-start(f32[2,256]{1,0:T(2,128)} %param.9) | copy-start | bytes 6148
  211.8 479.5 %copy-start = (bf16[2048,256]{1,0:T(8,128)(2,1)S(1)}, bf16[2048,256]{1,0:T(8,128)(2,1)}, u32[]{:S(2)}) copy-start(bf16[2048,256]{1,0:T(8,128)(2,1)} %param.8) | copy-start | bytes 3145732
Sparse Core Ops, SparseCore 0:
  10.0 119.7 all-gather.2
  133.0 78.7 all-gather.4
  217.8 471.6 all-reduce.1
where the time goes:
time: 703 us; the launch traced here: 702 us
  waiting for transfers between devices  498 us (71%)
  blocking collectives  95.3 us (14%)
  matrix products  64.5 us (9%)
  other arithmetic  25.3 us (4%)
  between operations  13.8 us (2%)
    psum x1, waiting for transfers between devices, local(): modal_csd = lax.psum(partial_csd, ('row', 'col'))  473 us
    all_gather x1, blocking collectives, local(): piece_points = lax.all_gather(coords, 'row', axis=1, tiled=True)  57.3 us
    dot_general x4, matrix products, add_block(): jnp.dot(part_shapes, coherence_tile, preferred_element_type=jnp.float32)  56.4 us
    all_gather x1, blocking collectives, local(): lax.all_gather(coords, 'col', axis=1, tiled=True)  37.9 us
    reduce_sum x4, other arithmetic, coherence(): squared = jnp.sum(difference * difference, axis=0)  25.3 us
    all_gather x1, waiting for transfers between devices, local(): piece_shapes = lax.all_gather(mode_shapes, 'row', axis=1, tiled=True)  23.6 us
  transfers between devices with their start and end apart: 3, of which 2 were waited for; matrix products, arithmetic and copies ran while one was open for 12% of the time, Pallas kernels for 0%

commit v1 on v0

v1 whole, which is shorter than its diff:
```python
import jax
import jax.numpy as jnp
from jax import lax
from jax.sharding import PartitionSpec as P

wave_scale = 0.35 / 64.0


def coherence(left_points, right_points):
    difference = left_points[:, :, None] - right_points[:, None, :]
    squared = jnp.sum(difference * difference, axis=0)
    return jnp.sinc(wave_scale * jnp.sqrt(squared)).astype(jnp.bfloat16)


def split_parts(matrix):
    high_part = matrix.astype(jnp.bfloat16)
    low_part = (matrix - high_part.astype(jnp.float32)).astype(jnp.bfloat16)
    return (high_part, low_part)


def pack_block(coords, mode_shapes):
    wide = coords.astype(jnp.float32)
    high = jnp.floor(wide * (1.0 / 256.0))
    low = wide - 256.0 * high
    pad = jnp.zeros((2, wide.shape[1]), jnp.float32)
    extra = jnp.concatenate([high, low, pad], axis=0).astype(jnp.bfloat16)
    return jnp.concatenate([mode_shapes, extra], axis=0)


def unpack_points(packed, mode_count):
    high = packed[..., mode_count:mode_count + 3, :].astype(jnp.float32)
    low = packed[..., mode_count + 3:mode_count + 6, :].astype(jnp.float32)
    return high * 256.0 + low


def gather_all(block, axis, count):
    spread = jnp.broadcast_to(block[None], (count,) + block.shape)
    return lax.all_to_all(spread, axis, 0, 0, tiled=True)


def all_reduce(matrix, rows, cols):
    flat = matrix.reshape(cols, -1)
    part = lax.all_to_all(flat, "col", 0, 0, tiled=True).reshape(cols, -1).sum(0)
    part = part.reshape(rows, -1)
    part = lax.all_to_all(part, "row", 0, 0, tiled=True).reshape(rows, -1).sum(0)
    whole = gather_all(part, "row", rows).reshape(-1)
    whole = gather_all(whole, "col", cols).reshape(-1)
    return whole.reshape(matrix.shape)


def local(coords, mode_shapes, output_shapes, response_gain):
    rows = lax.axis_size("row")
    cols = lax.axis_size("col")
    mode_count, block_nodes = mode_shapes.shape
    packed = pack_block(coords, mode_shapes)
    row_packed = gather_all(packed, "col", cols)
    col_packed = gather_all(packed, "row", rows)
    row_shapes = jnp.transpose(row_packed[:, :mode_count, :], (1, 0, 2)).reshape(mode_count, -1)
    row_points = jnp.transpose(unpack_points(row_packed, mode_count), (1, 0, 2)).reshape(3, -1)

    half = rows // 2
    me = lax.axis_index("row")
    order = (me + jnp.arange(half + 1)) % rows
    chosen = jnp.take(col_packed, order, axis=0)
    weights = jnp.where((jnp.arange(half + 1) == 0) | (jnp.arange(half + 1) == half), 0.5, 1.0)
    piece_shapes = (chosen[:, :mode_count, :] * weights[:, None, None].astype(jnp.bfloat16))
    piece_points = unpack_points(chosen, mode_count)

    def add_block(loop_index, running_sum):
        part_shapes = lax.dynamic_index_in_dim(piece_shapes, loop_index, 0, keepdims=False)
        part_points = lax.dynamic_index_in_dim(piece_points, loop_index, 0, keepdims=False)
        coherence_tile = coherence(part_points, row_points)
        return running_sum + jnp.dot(part_shapes, coherence_tile, preferred_element_type=jnp.float32)

    zero_block = jnp.zeros((mode_count, row_points.shape[1]), jnp.float32)
    projection = lax.fori_loop(0, half + 1, add_block, zero_block)
    high_part, low_part = split_parts(projection)
    dims = (((1,), (1,)), ((), ()))
    partial = lax.dot_general(row_shapes, high_part, dims, preferred_element_type=jnp.float32)
    partial = partial + lax.dot_general(row_shapes, low_part, dims, preferred_element_type=jnp.float32)
    total = all_reduce(partial, rows, cols)
    modal_csd = total + total.T
    real_part = response_gain[0]
    imag_part = response_gain[1]
    weighted = (
        real_part[:, None] * real_part[None, :] + imag_part[:, None] * imag_part[None, :]
    ) * modal_csd
    weighted_high, weighted_low = split_parts(weighted)
    mapped = jnp.dot(output_shapes, weighted_high, preferred_element_type=jnp.float32)
    mapped = mapped + jnp.dot(output_shapes, weighted_low, preferred_element_type=jnp.float32)
    response_power = jnp.sum(mapped * output_shapes.astype(jnp.float32), axis=1)
    return (response_power, modal_csd)


def solution(mesh):
    in_specs = (P(None, ("row", "col")), P(None, ("row", "col")), P(("row", "col"), None), P())
    out_specs = (P(("row", "col")), P())
    return jax.shard_map(local, mesh=mesh, in_specs=in_specs, out_specs=out_specs, check_vma=False)
```

time: 703 us -> 304 us (0.43)
  waiting for transfers between devices: 498 us -> 103 us
  blocking collectives: 95.3 us -> 74.1 us
  starting transfers between devices: 0.11 us -> 20.3 us
  matrix products: 64.5 us -> 83.1 us
  other arithmetic: 25.3 us -> 11.4 us
  between operations: 13.8 us -> 0.85 us
    psum x1 -> x0, waiting for transfers between devices: 473 us -> none  [local(): modal_csd = lax.psum(partial_csd, ('row', 'col'))]
    all_to_all x0 -> x2, waiting for transfers between devices: none -> 103 us  [gather_all(): return lax.all_to_all(spread, axis, 0, 0, tiled=True)]
    all_gather x2 -> x0, blocking collectives: 95.3 us -> none  [the longest x1 57.3 us: local(): piece_points = lax.all_gather(coords, 'row', axis=1, tiled=True)]
    all_to_all x0 -> x4, blocking collectives: none -> 74.1 us  [the longest x2 43.3 us: gather_all(): return lax.all_to_all(spread, axis, 0, 0, tiled=True)]
    all_gather x2 -> x0, waiting for transfers between devices: 23.6 us -> none  [the longest x1 23.6 us: local(): piece_shapes = lax.all_gather(mode_shapes, 'row', axis=1, tiled=True)]
    dot_general x4 -> x17, matrix products: 56.4 us -> 78.5 us  [add_block(): jnp.dot(part_shapes, coherence_tile, preferred_element_type=jnp.float32)]
    all_to_all x0 -> x2, starting transfers between devices: none -> 20.3 us  [gather_all(): return lax.all_to_all(spread, axis, 0, 0, tiled=True)]
    reduce_sum x4 -> x17, other arithmetic: 25.3 us -> 6.34 us  [coherence(): squared = jnp.sum(difference * difference, axis=0)]
  transfers between devices with their start and end apart: 3 -> 2, of which waited for: 2 -> 2; matrix products, arithmetic and copies ran while one was open for 12% -> 2% of each run, Pallas kernels for 0% -> 0%
where the time goes in v1:
time: 304 us; the launch traced here: 303 us
  waiting for transfers between devices  103 us (34%)
  matrix products  83.1 us (27%)
  blocking collectives  74.1 us (24%)
  starting transfers between devices  20.3 us (7%)
  other arithmetic  11.4 us (4%)
  local copies, waits for them, and re-layouts  9.78 us (3%)
    all_to_all x2, waiting for transfers between devices, gather_all(): return lax.all_to_all(spread, axis, 0, 0, tiled=True)  103 us
    dot_general x17, matrix products, add_block(): jnp.dot(part_shapes, coherence_tile, preferred_element_type=jnp.float32)  78.5 us
    all_to_all x2, blocking collectives, gather_all(): return lax.all_to_all(spread, axis, 0, 0, tiled=True)  43.3 us
    all_to_all x2, starting transfers between devices, gather_all(): return lax.all_to_all(spread, axis, 0, 0, tiled=True)  20.3 us
    all_to_all x1, blocking collectives, all_reduce(): lax.all_to_all(part, 'row', 0, 0, tiled=True).reshape(rows, -1).sum(0)  18.6 us
    all_to_all x1, blocking collectives, all_reduce(): lax.all_to_all(flat, 'col', 0, 0, tiled=True).reshape(cols, -1).sum(0)  12.3 us
    reduce_sum x17, other arithmetic, coherence(): squared = jnp.sum(difference * difference, axis=0)  6.34 us
  transfers between devices with their start and end apart: 2, of which 2 were waited for; matrix products, arithmetic and copies ran while one was open for 2% of the time, Pallas kernels for 0%

profile of v1, /device:TPU:1, one launch (start us, length us, event | category | flops | bytes accessed | tf_op | source)
XLA Modules:
  0.0 302.7 jit_solution(12252452037943667969)
XLA Ops:
  0.6 0.7 fusion.58
  1.3 0.1 pad.3.clone
  1.4 0.9 maximum_maximum_fusion
  2.3 0.1 broadcast_in_dim.73
  2.5 28.2 %all_to_all.41 = bf16[16,264,128]{2,1,0:T(8,128)(2,1)} all-to-all(bf16[16,264,128]{2,1,0:T(8,128)(2,1)S(1)} %broadcast_in_dim.73), channel_id=1, replica_groups=mesh['row'=32,'col'=16] {'col'}, dimensions={0} | all-to-all | bytes 2162688 | tf_op jit(solution)/shard_map/all_to_all | solution.py:38
  30.7 1.6 broadcast_in_dim.76
  32.4 13.6 %all-to-all-start.1 = ((bf16[32,264,128]{2,1,0:T(8,128)(2,1)}), bf16[32,264,128]{2,1,0:T(8,128)(2,1)S(1)}, u32[]{:S(2)}, u32[]{:S(2)}) async-start(bf16[32,264,128]{2,1,0:T(8,128)(2,1)} %broadcast_in_dim.76), calls=%async_computation.1 | async-start | bytes 4325376 | tf_op jit(solution)/shard_map/all_to_all | solution.py:38
  46.0 0.9 add_bitcast_fusion
  46.9 2.3 slice.34
  49.2 1.5 copy.30
  50.7 94.7 %all-to-all-done.1 = bf16[32,264,128]{2,1,0:T(8,128)(2,1)S(1)} async-done(((bf16[32,264,128]{2,1,0:T(8,128)(2,1)}), bf16[32,264,128]{2,1,0:T(8,128)(2,1)S(1)}, u32[]{:S(2)}, u32[]{:S(2)}) %all-to-all-start.1) | async-done | bytes 2162720 | tf_op jit(solution)/shard_map/all_to_all | solution.py:38
  145.4 1.8 gather_fusion
  147.2 1.6 broadcast_select_fusion
  148.8 0.1 slice_multiply_fusion
  148.9 85.4 %while.16 = (s32[]{:T(128)}, f32[256,2048]{1,0:T(8,128)}, bf16[17,256,128]{2,1,0:T(8,128)(2,1)S(1)}, f32[17,3,128]{2,1,0:T(4,128)S(1)}, f32[3,16,128]{2,1,0:T(8,128)S(1)}, /*index=5*/s32[]{:T(128)}, s32[]{:T(128)}) while((s32[]{:T(128)}, f32[256,2048]{1,0:T(8,128)}, bf16[17,256,128]{2,1,0:T(8,128)(2,1)S(1)}, ...), condition=%wide.region_2.3_spmd.clone, body=%wide.region_0.2_spmd.clone.sunk | while | flops 146538496 | bytes 6435423 | solution.py:76
  149.0 0.4 multiply_reduce_fusion.2
  149.4 3.1 %convolution_add_fusion.4 = f32[256,2048]{1,0:T(8,128)} fusion(f32[256,2048]{1,0:T(8,128)} %get-tuple-element.227, pred[]{:T(512)S(6)} %compare.11, f32[128,2048]{1,0:T(8,128)S(1)} %multiply_reduce_fusion.2, bf16[17,256,128]{2,1,0:T(8,128)(2,1)S(1)} %get-tuple-element.235, s32[]{:T(128)} %get-tuple-element.226), kind=kOutput, calls=%fused_computation.2.clone.1 | convolution fusion | flops 144441344 | bytes 5308421 | tf_op jit(solution)/shard_map/while/body/eval_jaxpr/dot_general | solution.py:73
  152.5 0.4 multiply_reduce_fusion.2
  152.9 4.7 %convolution_add_fusion.4 = f32[256,2048]{1,0:T(8,128)} fusion(f32[256,2048]{1,0:T(8,128)} %get-tuple-element.227, pred[]{:T(512)S(6)} %compare.11, f32[128,2048]{1,0:T(8,128)S(1)} %multiply_reduce_fusion.2, bf16[17,256,128]{2,1,0:T(8,128)(2,1)S(1)} %get-tuple-element.235, s32[]{:T(128)} %get-tuple-element.226), kind=kOutput, calls=%fused_computation.2.clone.1 | convolution fusion | flops 144441344 | bytes 5308421 | tf_op jit(solution)/shard_map/while/body/eval_jaxpr/dot_general | solution.py:73
  157.6 0.4 multiply_reduce_fusion.2
  158.0 4.7 %convolution_add_fusion.4 = f32[256,2048]{1,0:T(8,128)} fusion(f32[256,2048]{1,0:T(8,128)} %get-tuple-element.227, pred[]{:T(512)S(6)} %compare.11, f32[128,2048]{1,0:T(8,128)S(1)} %multiply_reduce_fusion.2, bf16[17,256,128]{2,1,0:T(8,128)(2,1)S(1)} %get-tuple-element.235, s32[]{:T(128)} %get-tuple-element.226), kind=kOutput, calls=%fused_computation.2.clone.1 | convolution fusion | flops 144441344 | bytes 5308421 | tf_op jit(solution)/shard_map/while/body/eval_jaxpr/dot_general | solution.py:73
  162.8 0.4 multiply_reduce_fusion.2
  163.1 4.7 %convolution_add_fusion.4 = f32[256,2048]{1,0:T(8,128)} fusion(f32[256,2048]{1,0:T(8,128)} %get-tuple-element.227, pred[]{:T(512)S(6)} %compare.11, f32[128,2048]{1,0:T(8,128)S(1)} %multiply_reduce_fusion.2, bf16[17,256,128]{2,1,0:T(8,128)(2,1)S(1)} %get-tuple-element.235, s32[]{:T(128)} %get-tuple-element.226), kind=kOutput, calls=%fused_computation.2.clone.1 | convolution fusion | flops 144441344 | bytes 5308421 | tf_op jit(solution)/shard_map/while/body/eval_jaxpr/dot_general | solution.py:73
  167.9 0.4 multiply_reduce_fusion.2
  168.3 4.7 %convolution_add_fusion.4 = f32[256,2048]{1,0:T(8,128)} fusion(f32[256,2048]{1,0:T(8,128)} %get-tuple-element.227, pred[]{:T(512)S(6)} %compare.11, f32[128,2048]{1,0:T(8,128)S(1)} %multiply_reduce_fusion.2, bf16[17,256,128]{2,1,0:T(8,128)(2,1)S(1)} %get-tuple-element.235, s32[]{:T(128)} %get-tuple-element.226), kind=kOutput, calls=%fused_computation.2.clone.1 | convolution fusion | flops 144441344 | bytes 5308421 | tf_op jit(solution)/shard_map/while/body/eval_jaxpr/dot_general | solution.py:73
  173.0 0.4 multiply_reduce_fusion.2
  173.4 4.7 %convolution_add_fusion.4 = f32[256,2048]{1,0:T(8,128)} fusion(f32[256,2048]{1,0:T(8,128)} %get-tuple-element.227, pred[]{:T(512)S(6)} %compare.11, f32[128,2048]{1,0:T(8,128)S(1)} %multiply_reduce_fusion.2, bf16[17,256,128]{2,1,0:T(8,128)(2,1)S(1)} %get-tuple-element.235, s32[]{:T(128)} %get-tuple-element.226), kind=kOutput, calls=%fused_computation.2.clone.1 | convolution fusion | flops 144441344 | bytes 5308421 | tf_op jit(solution)/shard_map/while/body/eval_jaxpr/dot_general | solution.py:73
  178.1 0.4 multiply_reduce_fusion.2
  178.5 4.7 %convolution_add_fusion.4 = f32[256,2048]{1,0:T(8,128)} fusion(f32[256,2048]{1,0:T(8,128)} %get-tuple-element.227, pred[]{:T(512)S(6)} %compare.11, f32[128,2048]{1,0:T(8,128)S(1)} %multiply_reduce_fusion.2, bf16[17,256,128]{2,1,0:T(8,128)(2,1)S(1)} %get-tuple-element.235, s32[]{:T(128)} %get-tuple-element.226), kind=kOutput, calls=%fused_computation.2.clone.1 | convolution fusion | flops 144441344 | bytes 5308421 | tf_op jit(solution)/shard_map/while/body/eval_jaxpr/dot_general | solution.py:73
  183.2 0.4 multiply_reduce_fusion.2
  183.6 4.7 %convolution_add_fusion.4 = f32[256,2048]{1,0:T(8,128)} fusion(f32[256,2048]{1,0:T(8,128)} %get-tuple-element.227, pred[]{:T(512)S(6)} %compare.11, f32[128,2048]{1,0:T(8,128)S(1)} %multiply_reduce_fusion.2, bf16[17,256,128]{2,1,0:T(8,128)(2,1)S(1)} %get-tuple-element.235, s32[]{:T(128)} %get-tuple-element.226), kind=kOutput, calls=%fused_computation.2.clone.1 | convolution fusion | flops 144441344 | bytes 5308421 | tf_op jit(solution)/shard_map/while/body/eval_jaxpr/dot_general | solution.py:73
  188.3 0.4 multiply_reduce_fusion.2
  188.7 4.7 %convolution_add_fusion.4 = f32[256,2048]{1,0:T(8,128)} fusion(f32[256,2048]{1,0:T(8,128)} %get-tuple-element.227, pred[]{:T(512)S(6)} %compare.11, f32[128,2048]{1,0:T(8,128)S(1)} %multiply_reduce_fusion.2, bf16[17,256,128]{2,1,0:T(8,128)(2,1)S(1)} %get-tuple-element.235, s32[]{:T(128)} %get-tuple-element.226), kind=kOutput, calls=%fused_computation.2.clone.1 | convolution fusion | flops 144441344 | bytes 5308421 | tf_op jit(solution)/shard_map/while/body/eval_jaxpr/dot_general | solution.py:73
  193.5 0.4 multiply_reduce_fusion.2
  193.9 4.7 %convolution_add_fusion.4 = f32[256,2048]{1,0:T(8,128)} fusion(f32[256,2048]{1,0:T(8,128)} %get-tuple-element.227, pred[]{:T(512)S(6)} %compare.11, f32[128,2048]{1,0:T(8,128)S(1)} %multiply_reduce_fusion.2, bf16[17,256,128]{2,1,0:T(8,128)(2,1)S(1)} %get-tuple-element.235, s32[]{:T(128)} %get-tuple-element.226), kind=kOutput, calls=%fused_computation.2.clone.1 | convolution fusion | flops 144441344 | bytes 5308421 | tf_op jit(solution)/shard_map/while/body/eval_jaxpr/dot_general | solution.py:73
  198.6 0.4 multiply_reduce_fusion.2
  199.0 4.7 %convolution_add_fusion.4 = f32[256,2048]{1,0:T(8,128)} fusion(f32[256,2048]{1,0:T(8,128)} %get-tuple-element.227, pred[]{:T(512)S(6)} %compare.11, f32[128,2048]{1,0:T(8,128)S(1)} %multiply_reduce_fusion.2, bf16[17,256,128]{2,1,0:T(8,128)(2,1)S(1)} %get-tuple-element.235, s32[]{:T(128)} %get-tuple-element.226), kind=kOutput, calls=%fused_computation.2.clone.1 | convolution fusion | flops 144441344 | bytes 5308421 | tf_op jit(solution)/shard_map/while/body/eval_jaxpr/dot_general | solution.py:73
  203.7 0.4 multiply_reduce_fusion.2
  204.1 4.7 %convolution_add_fusion.4 = f32[256,2048]{1,0:T(8,128)} fusion(f32[256,2048]{1,0:T(8,128)} %get-tuple-element.227, pred[]{:T(512)S(6)} %compare.11, f32[128,2048]{1,0:T(8,128)S(1)} %multiply_reduce_fusion.2, bf16[17,256,128]{2,1,0:T(8,128)(2,1)S(1)} %get-tuple-element.235, s32[]{:T(128)} %get-tuple-element.226), kind=kOutput, calls=%fused_computation.2.clone.1 | convolution fusion | flops 144441344 | bytes 5308421 | tf_op jit(solution)/shard_map/while/body/eval_jaxpr/dot_general | solution.py:73
  208.8 0.4 multiply_reduce_fusion.2
  209.2 4.7 %convolution_add_fusion.4 = f32[256,2048]{1,0:T(8,128)} fusion(f32[256,2048]{1,0:T(8,128)} %get-tuple-element.227, pred[]{:T(512)S(6)} %compare.11, f32[128,2048]{1,0:T(8,128)S(1)} %multiply_reduce_fusion.2, bf16[17,256,128]{2,1,0:T(8,128)(2,1)S(1)} %get-tuple-element.235, s32[]{:T(128)} %get-tuple-element.226), kind=kOutput, calls=%fused_computation.2.clone.1 | convolution fusion | flops 144441344 | bytes 5308421 | tf_op jit(solution)/shard_map/while/body/eval_jaxpr/dot_general | solution.py:73
  213.9 0.4 multiply_reduce_fusion.2
  214.3 4.7 %convolution_add_fusion.4 = f32[256,2048]{1,0:T(8,128)} fusion(f32[256,2048]{1,0:T(8,128)} %get-tuple-element.227, pred[]{:T(512)S(6)} %compare.11, f32[128,2048]{1,0:T(8,128)S(1)} %multiply_reduce_fusion.2, bf16[17,256,128]{2,1,0:T(8,128)(2,1)S(1)} %get-tuple-element.235, s32[]{:T(128)} %get-tuple-element.226), kind=kOutput, calls=%fused_computation.2.clone.1 | convolution fusion | flops 144441344 | bytes 5308421 | tf_op jit(solution)/shard_map/while/body/eval_jaxpr/dot_general | solution.py:73
  219.1 0.4 multiply_reduce_fusion.2
  219.4 4.7 %convolution_add_fusion.4 = f32[256,2048]{1,0:T(8,128)} fusion(f32[256,2048]{1,0:T(8,128)} %get-tuple-element.227, pred[]{:T(512)S(6)} %compare.11, f32[128,2048]{1,0:T(8,128)S(1)} %multiply_reduce_fusion.2, bf16[17,256,128]{2,1,0:T(8,128)(2,1)S(1)} %get-tuple-element.235, s32[]{:T(128)} %get-tuple-element.226), kind=kOutput, calls=%fused_computation.2.clone.1 | convolution fusion | flops 144441344 | bytes 5308421 | tf_op jit(solution)/shard_map/while/body/eval_jaxpr/dot_general | solution.py:73
  224.2 0.4 multiply_reduce_fusion.2
  224.6 4.7 %convolution_add_fusion.4 = f32[256,2048]{1,0:T(8,128)} fusion(f32[256,2048]{1,0:T(8,128)} %get-tuple-element.227, pred[]{:T(512)S(6)} %compare.11, f32[128,2048]{1,0:T(8,128)S(1)} %multiply_reduce_fusion.2, bf16[17,256,128]{2,1,0:T(8,128)(2,1)S(1)} %get-tuple-element.235, s32[]{:T(128)} %get-tuple-element.226), kind=kOutput, calls=%fused_computation.2.clone.1 | convolution fusion | flops 144441344 | bytes 5308421 | tf_op jit(solution)/shard_map/while/body/eval_jaxpr/dot_general | solution.py:73
  229.3 0.4 multiply_reduce_fusion.2
  229.7 4.7 %convolution_add_fusion.4 = f32[256,2048]{1,0:T(8,128)} fusion(f32[256,2048]{1,0:T(8,128)} %get-tuple-element.227, pred[]{:T(512)S(6)} %compare.11, f32[128,2048]{1,0:T(8,128)S(1)} %multiply_reduce_fusion.2, bf16[17,256,128]{2,1,0:T(8,128)(2,1)S(1)} %get-tuple-element.235, s32[]{:T(128)} %get-tuple-element.226), kind=kOutput, calls=%fused_computation.2.clone.1 | convolution fusion | flops 144441344 | bytes 5308421 | tf_op jit(solution)/shard_map/while/body/eval_jaxpr/dot_general | solution.py:73
  234.4 2.2 fusion.45
  236.6 0.5 convolution_add_fusion.2
  237.1 0.3 all_to_all.34
  237.4 12.3 %all_to_all.42 = f32[16,1,4096]{2,1,0:T(1,128)S(1)} all-to-all(f32[16,1,4096]{2,1,0:T(1,128)S(1)} %all_to_all.34), channel_id=1, replica_groups=mesh['row'=32,'col'=16] {'col'}, dimensions={0} | all-to-all | bytes 524288 | tf_op jit(solution)/shard_map/all_to_all | solution.py:43
  249.7 0.2 reduce_sum.43
  249.9 18.6 %all_to_all.43 = f32[32,1,128]{2,1,0:T(1,128)S(1)} all-to-all(f32[32,1,128]{2,1,0:T(1,128)S(1)} %bitcast.45), channel_id=1, replica_groups=mesh['row'=32,'col'=16] {'row'}, dimensions={0} | all-to-all | bytes 32768 | tf_op jit(solution)/shard_map/all_to_all | solution.py:45
  268.5 15.0 %all_to_all.44 = f32[32,1,128]{2,1,0:T(1,128)S(1)} all-to-all(f32[32,1,128]{2,1,0:T(1,128)S(1)} %broadcast_in_dim.80), channel_id=1, replica_groups=mesh['row'=32,'col'=16] {'row'}, dimensions={0} | all-to-all | bytes 32768 | tf_op jit(solution)/shard_map/all_to_all | solution.py:38
  283.5 0.9 broadcast_in_dim.82
  284.4 6.7 %all-to-all-start.5 = ((f32[16,1,4096]{2,1,0:T(1,128)}), f32[16,1,4096]{2,1,0:T(1,128)S(1)}, u32[]{:S(2)}, u32[]{:S(2)}) async-start(f32[16,1,4096]{2,1,0:T(1,128)} %broadcast_in_dim.82), calls=%async_computation.5 | async-start | bytes 524288 | tf_op jit(solution)/shard_map/all_to_all | solution.py:38
  291.2 0.6 copy.29
  291.8 8.1 %all-to-all-done.5 = f32[16,1,4096]{2,1,0:T(1,128)S(1)} async-done(((f32[16,1,4096]{2,1,0:T(1,128)}), f32[16,1,4096]{2,1,0:T(1,128)S(1)}, u32[]{:S(2)}, u32[]{:S(2)}) %all-to-all-start.5) | async-done | bytes 262176 | tf_op jit(solution)/shard_map/all_to_all | solution.py:38
  299.9 0.6 reduce.2
  300.6 0.1 copy.28
  300.8 0.6 fusion.48
  301.4 1.3 fusion.43
  (55 shorter events, 0.5 us)
Async XLA Ops:
  32.4 113.0 %all-to-all-start.1 = ((bf16[32,264,128]{2,1,0:T(8,128)(2,1)}), bf16[32,264,128]{2,1,0:T(8,128)(2,1)S(1)}, u32[]{:S(2)}, u32[]{:S(2)}) async-start(bf16[32,264,128]{2,1,0:T(8,128)(2,1)} %broadcast_in_dim.76), calls=%async_computation.1 | async-start | bytes 4325376 | tf_op jit(solution)/shard_map/all_to_all | solution.py:38
  234.4 2.2 copy-start.1
  236.6 54.5 %copy-start = (bf16[2048,256]{1,0:T(8,128)(2,1)S(1)}, bf16[2048,256]{1,0:T(8,128)(2,1)}, u32[]{:S(2)}) copy-start(bf16[2048,256]{1,0:T(8,128)(2,1)} %param.8) | copy-start | bytes 3145732
  237.1 54.7 %copy-start.3 = (f32[2,256]{1,0:T(2,128)S(1)}, f32[2,256]{1,0:T(2,128)}, u32[]{:S(2)}) copy-start(f32[2,256]{1,0:T(2,128)} %param.9) | copy-start | bytes 6148
  284.4 15.5 %all-to-all-start.5 = ((f32[16,1,4096]{2,1,0:T(1,128)}), f32[16,1,4096]{2,1,0:T(1,128)S(1)}, u32[]{:S(2)}, u32[]{:S(2)}) async-start(f32[16,1,4096]{2,1,0:T(1,128)} %broadcast_in_dim.82), calls=%async_computation.5 | async-start | bytes 524288 | tf_op jit(solution)/shard_map/all_to_all | solution.py:38
  300.8 1.9 copy-start.2
